TPU v7x, 256 devices: a whole 4x4x8 slice. The times are simulated.
256 devices in a mesh: col: 32 (over x, y, core), row: 8 (over z).
Axes of the slice: x: 4, y: 4, z: 8, core: 2. Of those that a mesh axis runs over, the one named last changes fastest.
Arguments:
- weights: float32 [4096, 53248], P('row', 'col'), may hold values from -6 to 6
- factor: float32 [6, 512, 53248], P(None, 'row', 'col'), as said below
- diag_inverse: float32 [6, 4, 128, 128], replicated
- prune_mask: int32 [6, 32, 4], P(None, 'row'), may hold values 0 or 1
- panel_start: int32 [6], replicated, may hold values from 0 to 52736, as said below
Outputs:
- pruned: float32 [4096, 53248], P('row', 'col')
Inputs may be any that keep to these rules, and one draw needn't show every extreme that they name: `panel_start`: strictly increasing; each a multiple of 128; each panel lies within one block of 1664 columns, and no two panels in the same block. `factor`: row j of panel k is zero left of column panel_start[k] + j and positive on it.
All inputs are finite; a program needn't handle non-finite values. No bound on the sum of `prune_mask` on one device may be relied on, other than what follows from the above.
Results may differ from a plain program's by a relative error of at most 0.0001.
Values sent between devices are 32-bit elements; how exact they have to be, the bound alone decides.
No kernel may reach another device: no remote copies, remote signals or barrier semaphores. Data moves between devices by JAX's collectives and lax.ppermute only.
A program may use at most 192 MiB of HBM per device.

v0:
```python
import jax
import jax.numpy as jnp
from jax import lax
from jax.sharding import Mesh
from jax.sharding import PartitionSpec as P

TILE = 128
PANEL_TILES = 4
PW = 512
P_SIZE = 6
COL = ("col_0", "col_1", "col_2")


def cut_along(value, dim, devices):
    dims = value.shape
    tiles = value.reshape(*dims[:dim], devices, dims[dim] // devices, *dims[dim + 1 :])
    return jnp.moveaxis(tiles, dim, 0)


def sent_and_summed(value, axis, dim):
    tiles = cut_along(value, dim, lax.axis_size(axis))
    arrived = lax.all_to_all(tiles, axis, split_axis=0, concat_axis=0, tiled=True)
    return arrived.sum(axis=0)


def summed_rows(value, axes, dim):
    far, near = axes
    own = sent_and_summed(cut_along(value, dim, lax.axis_size(far)), near, dim + 1)
    return jnp.sum(lax.all_to_all(own, far, 0, 0, tiled=True), axis=0)


def filled_up(lines, devices):
    spare = -lines.shape[0] % devices
    if not spare:
        return lines
    return jnp.concatenate([lines, jnp.zeros((spare, *lines.shape[1:]), lines.dtype)])


def sent_to_all(value, axis):
    devices = lax.axis_size(axis)
    return lax.all_to_all(
        jnp.broadcast_to(value[None], (devices, *value.shape)), axis, 0, 0, tiled=True
    )


def laid_out(tiles, dim):
    dims = list(tiles.shape[1:])
    dims[dim] *= tiles.shape[0]
    return jnp.moveaxis(tiles, 0, dim).reshape(dims)


def gathered_by_axis(value, axes, dim):
    far, near = axes
    leading = sent_to_all(value, far)
    tiles = jnp.swapaxes(sent_to_all(leading, near), 0, 1)
    return laid_out(tiles.reshape(-1, *value.shape), dim)


def nested_sum(value, axes):
    lines = value.reshape(-1, value.shape[-1])
    own = summed_rows(filled_up(lines, lax.axis_size(axes[0]) * lax.axis_size(axes[1])), axes, 0)
    whole = gathered_by_axis(own, axes, 0)
    return whole[: len(lines)].reshape(value.shape)


def panel_errors(wpanel, ublock, dinv, rowmask):
    tiles = []
    for a in range(PANEL_TILES):
        acc = wpanel[:, a * TILE : (a + 1) * TILE]
        for b in range(a):
            acc = acc - jnp.dot(
                tiles[b],
                ublock[b * TILE : (b + 1) * TILE, a * TILE : (a + 1) * TILE],
                precision=lax.Precision.HIGHEST,
            )
        tiles.append(rowmask[:, a : a + 1] * jnp.dot(acc, dinv[a], precision=lax.Precision.HIGHEST))
    return jnp.concatenate(tiles, 1)


def shards(weights, factor, diag_inverse, prune_mask, panel_start):
    width = weights.shape[1]
    myself = lax.axis_index(COL)
    starts = TILE * jnp.arange(PANEL_TILES, dtype=jnp.int32)
    all_rows = lax.all_gather(factor, "row", axis=1, tiled=True)
    for k in range(P_SIZE):
        first = panel_start[k]
        owner = first // width
        shift_col = jnp.clip(first - myself * width, 0, width - PW)
        wpanel = lax.dynamic_slice_in_dim(weights, shift_col, PW, 1)
        rows_k = all_rows[k]
        ublock = lax.dynamic_slice_in_dim(rows_k, shift_col, PW, 1)
        rowmask = jnp.repeat(prune_mask[k].astype(jnp.float32), TILE, axis=0)
        errors = panel_errors(wpanel, ublock, diag_inverse[k], rowmask)
        owned = jnp.where(myself == owner, errors, jnp.zeros_like(errors))
        errors = nested_sum(owned, (("col_0", "col_1"), "col_2"))
        weights = weights - jnp.dot(errors, rows_k, precision=lax.Precision.HIGHEST)
        offset = myself * width + jnp.arange(width, dtype=jnp.int32) - first
        indicator = (
            (offset[None, :] >= starts[:, None]) & (offset[None, :] < starts[:, None] + TILE)
        ).astype(jnp.float32)
        prune = jnp.dot(rowmask, indicator, precision=lax.Precision.HIGHEST)
        weights = weights * (1.0 - prune)
    return weights


def solution(mesh):
    torus = Mesh(
        mesh.devices.reshape(4, 4, 2, mesh.shape["row"]), ("col_0", "col_1", "col_2", "row")
    )
    return jax.shard_map(
        shards,
        mesh=torus,
        in_specs=(P("row", COL), P(None, "row", COL), P(), P(None, "row", None), P()),
        out_specs=P("row", COL),
        check_vma=False,
    )
```

profile of v0, /device:TPU:1, one launch (start us, length us, event | category | flops | bytes accessed | tf_op | source)
XLA Modules:
  0.0 636.6 jit_solution(11401464521342157056)
XLA Ops:
  14.8 205.2 %all-gather.2.cloned.1.call-done = f32[6,512,1664]{2,1,0:T(8,128)} async-done(((f32[6,64,1664]{2,1,0:T(8,128)}), f32[6,512,1664]{2,1,0:T(8,128)}) %all-gather.2.cloned.1.call-update) | async-done | bytes 20447248 | tf_op jit(solution)/shard_map/all_gather | solution.py:84
  219.9 12.4 %fusion.180 = (f32[1,512,1664]{2,1,0:T(8,128)}, f32[1,512,1664]{2,1,0:T(8,128)}, f32[1,512,1664]{2,1,0:T(8,128)}, f32[1,512,1664]{2,1,0:T(8,128)}, f32[1,512,1664]{2,1,0:T(8,128)S(1)}, /*index=5*/f32[1,512,1664]{2,1,0:T(8,128)S(1)}) fusion(f32[6,512,1664]{2,1,0:T(8,128)} %all-gather.2.cloned.1.call-done), kind=kLoop, calls=%fused_computation.273 | loop fusion | bytes 40894464 | tf_op jit(solution)/shard_map/slice | solution.py:90
  248.9 6.5 %all-to-all-start.1 = ((f32[16,16,512]{2,1,0:T(8,128)}), f32[16,16,512]{2,1,0:T(8,128)S(1)}, u32[]{:S(2)}, u32[]{:S(2)}) async-start(f32[16,16,512]{2,1,0:T(8,128)} %reduce_sum.108), calls=%async_computation.1 | async-start | bytes 1048576 | tf_op jit(solution)/shard_map/all_to_all | solution.py:29
  258.4 7.5 %all-to-all-done.1 = f32[16,16,512]{2,1,0:T(8,128)S(1)} async-done(((f32[16,16,512]{2,1,0:T(8,128)}), f32[16,16,512]{2,1,0:T(8,128)S(1)}, u32[]{:S(2)}, u32[]{:S(2)}) %all-to-all-start.1) | async-done | bytes 524320 | tf_op jit(solution)/shard_map/all_to_all | solution.py:29
  273.8 5.9 all-to-all-done.2
  279.8 8.2 %all_to_all.121 = f32[2,16,16,512]{3,2,1,0:T(8,128)S(1)} all-to-all(f32[2,16,16,512]{3,2,1,0:T(8,128)S(1)} %broadcast_in_dim.38), channel_id=1, replica_groups=mesh['col_0'=4,'col_1'=4,'col_2'=2,'row'=8] {'col_2'}, dimensions={0} | all-to-all | bytes 2097152 | tf_op jit(solution)/shard_map/all_to_all | solution.py:41
  288.1 9.1 %bitcast_multiply_fusion.5 = f32[512,1664]{1,0:T(8,128)S(1)} fusion(f32[1664,512]{0,1:T(8,128)S(1)} %copy-done.8, f32[512,1664]{1,0:T(8,128)} %param.5, f32[512,512]{1,0:T(8,128)S(1)} %bitcast.335, f32[6,512,1664]{2,1,0:T(8,128)} %all-gather.2.cloned.1.call-done), kind=kOutput, calls=%fused_computation.15 | convolution fusion | flops 5237047296 | bytes 14680064 | tf_op jit(solution)/shard_map/dot_general | solution.py:96
  321.5 10.0 %all-to-all-done.5 = f32[16,16,512]{2,1,0:T(8,128)} async-done(((f32[16,16,512]{2,1,0:T(8,128)}), f32[16,16,512]{2,1,0:T(8,128)}, u32[]{:S(2)}, u32[]{:S(2)}) %all-to-all-start.5) | async-done | bytes 524320 | tf_op jit(solution)/shard_map/all_to_all | solution.py:29
  350.0 6.4 %all_to_all.123 = f32[2,16,16,512]{3,2,1,0:T(8,128)S(1)} all-to-all(f32[2,16,16,512]{3,2,1,0:T(8,128)S(1)} %broadcast_in_dim.41), channel_id=1, replica_groups=mesh['col_0'=4,'col_1'=4,'col_2'=2,'row'=8] {'col_2'}, dimensions={0} | all-to-all | bytes 2097152 | tf_op jit(solution)/shard_map/all_to_all | solution.py:41
  356.5 8.1 %bitcast_multiply_fusion.4 = f32[512,1664]{1,0:T(8,128)S(1)} fusion(f32[1664,512]{0,1:T(8,128)S(1)} %copy-done.7, f32[512,1664]{1,0:T(8,128)S(1)} %bitcast_multiply_fusion.5, f32[512,512]{1,0:T(8,128)S(1)} %bitcast.331, f32[6,512,1664]{2,1,0:T(8,128)} %all-gather.2.cloned.1.call-done), kind=kOutput, calls=%fused_computation.12 | convolution fusion | flops 5237047296 | bytes 14680064 | tf_op jit(solution)/shard_map/dot_general | solution.py:96
  382.5 7.5 %all-to-all-start.9 = ((f32[16,16,512]{2,1,0:T(8,128)}), f32[16,16,512]{2,1,0:T(8,128)S(1)}, u32[]{:S(2)}, u32[]{:S(2)}) async-start(f32[16,16,512]{2,1,0:T(8,128)} %reduce_sum.112), calls=%async_computation.9 | async-start | bytes 1048576 | tf_op jit(solution)/shard_map/all_to_all | solution.py:29
  392.8 7.6 %all-to-all-done.9 = f32[16,16,512]{2,1,0:T(8,128)S(1)} async-done(((f32[16,16,512]{2,1,0:T(8,128)}), f32[16,16,512]{2,1,0:T(8,128)S(1)}, u32[]{:S(2)}, u32[]{:S(2)}) %all-to-all-start.9) | async-done | bytes 524320 | tf_op jit(solution)/shard_map/all_to_all | solution.py:29
  414.4 7.7 %all_to_all.125 = f32[2,16,16,512]{3,2,1,0:T(8,128)S(1)} all-to-all(f32[2,16,16,512]{3,2,1,0:T(8,128)S(1)} %broadcast_in_dim.44), channel_id=1, replica_groups=mesh['col_0'=4,'col_1'=4,'col_2'=2,'row'=8] {'col_2'}, dimensions={0} | all-to-all | bytes 2097152 | tf_op jit(solution)/shard_map/all_to_all | solution.py:41
  422.2 9.1 %bitcast_multiply_fusion.3 = f32[512,1664]{1,0:T(8,128)S(1)} fusion(f32[1664,512]{0,1:T(8,128)} %fusion.132, f32[512,1664]{1,0:T(8,128)S(1)} %copy-done.3, f32[512,512]{1,0:T(8,128)S(1)} %bitcast.332, f32[6,512,1664]{2,1,0:T(8,128)} %all-gather.2.cloned.1.call-done), kind=kOutput, calls=%fused_computation.9 | convolution fusion | flops 5237047296 | bytes 14680064 | tf_op jit(solution)/shard_map/dot_general | solution.py:96
  455.5 10.0 %all-to-all-done.13 = f32[16,16,512]{2,1,0:T(8,128)} async-done(((f32[16,16,512]{2,1,0:T(8,128)}), f32[16,16,512]{2,1,0:T(8,128)}, u32[]{:S(2)}, u32[]{:S(2)}) %all-to-all-start.13) | async-done | bytes 524320 | tf_op jit(solution)/shard_map/all_to_all | solution.py:29
  483.3 6.6 %all_to_all.127 = f32[2,16,16,512]{3,2,1,0:T(8,128)S(1)} all-to-all(f32[2,16,16,512]{3,2,1,0:T(8,128)S(1)} %broadcast_in_dim.47), channel_id=1, replica_groups=mesh['col_0'=4,'col_1'=4,'col_2'=2,'row'=8] {'col_2'}, dimensions={0} | all-to-all | bytes 2097152 | tf_op jit(solution)/shard_map/all_to_all | solution.py:41
  490.1 8.1 %bitcast_multiply_fusion.2 = f32[512,1664]{1,0:T(8,128)S(1)} fusion(f32[1664,512]{0,1:T(8,128)S(1)} %copy-done.6, f32[512,1664]{1,0:T(8,128)S(1)} %bitcast_multiply_fusion.3, f32[512,512]{1,0:T(8,128)S(1)} %bitcast.333, f32[6,512,1664]{2,1,0:T(8,128)} %all-gather.2.cloned.1.call-done), kind=kOutput, calls=%fused_computation.6 | convolution fusion | flops 5237047296 | bytes 14680064 | tf_op jit(solution)/shard_map/dot_general | solution.py:96
  516.0 6.8 %all-to-all-start.17 = ((f32[16,16,512]{2,1,0:T(8,128)}), f32[16,16,512]{2,1,0:T(8,128)S(1)}, u32[]{:S(2)}, u32[]{:S(2)}) async-start(f32[16,16,512]{2,1,0:T(8,128)} %reduce_sum.116), calls=%async_computation.17 | async-start | bytes 1048576 | tf_op jit(solution)/shard_map/all_to_all | solution.py:29
  525.3 7.9 %all-to-all-done.17 = f32[16,16,512]{2,1,0:T(8,128)S(1)} async-done(((f32[16,16,512]{2,1,0:T(8,128)}), f32[16,16,512]{2,1,0:T(8,128)S(1)}, u32[]{:S(2)}, u32[]{:S(2)}) %all-to-all-start.17) | async-done | bytes 524320 | tf_op jit(solution)/shard_map/all_to_all | solution.py:29
  548.7 7.7 %all_to_all.129 = f32[2,16,16,512]{3,2,1,0:T(8,128)S(1)} all-to-all(f32[2,16,16,512]{3,2,1,0:T(8,128)S(1)} %broadcast_in_dim.50), channel_id=1, replica_groups=mesh['col_0'=4,'col_1'=4,'col_2'=2,'row'=8] {'col_2'}, dimensions={0} | all-to-all | bytes 2097152 | tf_op jit(solution)/shard_map/all_to_all | solution.py:41
  556.5 9.1 %bitcast_multiply_fusion.1 = f32[512,1664]{1,0:T(8,128)S(1)} fusion(f32[1664,512]{0,1:T(8,128)} %fusion.124, f32[512,1664]{1,0:T(8,128)S(1)} %copy-done.1, f32[512,512]{1,0:T(8,128)S(1)} %bitcast.334, f32[6,512,1664]{2,1,0:T(8,128)} %all-gather.2.cloned.1.call-done), kind=kOutput, calls=%fused_computation.3 | convolution fusion | flops 5237047296 | bytes 14680064 | tf_op jit(solution)/shard_map/dot_general | solution.py:96
  582.6 13.3 %all_to_all.131 = f32[16,16,512]{2,1,0:T(8,128)S(1)} all-to-all(f32[16,16,512]{2,1,0:T(8,128)S(1)} %reduce_sum.118), channel_id=1, replica_groups=mesh['col_0'=4,'col_1'=4,'col_2'=2,'row'=8] {'col_0','col_1'}, dimensions={0} | all-to-all | bytes 1048576 | tf_op jit(solution)/shard_map/all_to_all | solution.py:29
  611.5 7.7 %all_to_all.132 = f32[2,16,16,512]{3,2,1,0:T(8,128)S(1)} all-to-all(f32[2,16,16,512]{3,2,1,0:T(8,128)S(1)} %broadcast_in_dim.53), channel_id=1, replica_groups=mesh['col_0'=4,'col_1'=4,'col_2'=2,'row'=8] {'col_2'}, dimensions={0} | all-to-all | bytes 2097152 | tf_op jit(solution)/shard_map/all_to_all | solution.py:41
  619.3 10.2 %bitcast_multiply_fusion = f32[512,1664]{1,0:T(8,128)} fusion(f32[1664,512]{0,1:T(8,128)} %fusion.120, f32[512,1664]{1,0:T(8,128)S(1)} %copy-done.5, f32[512,512]{1,0:T(8,128)S(1)} %bitcast.330, f32[6,512,1664]{2,1,0:T(8,128)} %all-gather.2.cloned.1.call-done), kind=kOutput, calls=%fused_computation | convolution fusion | flops 5237047296 | bytes 14680064 | tf_op jit(solution)/shard_map/dot_general | solution.py:96
  (177 shorter events, 208.4 us)
Async XLA Ops:
  6.5 213.4 %all-gather.2.cloned.1.call-start = ((), (), s32[]{:S(2)}) async-start(), calls=%async_computation.24 | async-start | bytes 23003136 | tf_op jit(solution)/shard_map/all_gather | solution.py:84
  248.9 16.9 %all-to-all-start.1 = ((f32[16,16,512]{2,1,0:T(8,128)}), f32[16,16,512]{2,1,0:T(8,128)S(1)}, u32[]{:S(2)}, u32[]{:S(2)}) async-start(f32[16,16,512]{2,1,0:T(8,128)} %reduce_sum.108), calls=%async_computation.1 | async-start | bytes 1048576 | tf_op jit(solution)/shard_map/all_to_all | solution.py:29
  266.7 13.0 %all-to-all-start.2 = ((f32[16,16,512]{2,1,0:T(8,128)}), f32[16,16,512]{2,1,0:T(8,128)S(1)}, u32[]{:S(2)}, u32[]{:S(2)}) async-start(f32[16,16,512]{2,1,0:T(8,128)} %broadcast_in_dim.37), calls=%async_computation.2 | async-start | bytes 1048576 | tf_op jit(solution)/shard_map/all_to_all | solution.py:41
  279.7 8.4 %copy-start.8 = (f32[1664,512]{0,1:T(8,128)S(1)}, f32[1664,512]{0,1:T(8,128)}, u32[]{:S(2)}) copy-start(f32[1664,512]{0,1:T(8,128)} %fusion.140) | copy-start | bytes 10223620
  317.1 14.5 %all-to-all-start.5 = ((f32[16,16,512]{2,1,0:T(8,128)}), f32[16,16,512]{2,1,0:T(8,128)}, u32[]{:S(2)}, u32[]{:S(2)}) async-start(f32[16,16,512]{2,1,0:T(8,128)} %reduce_sum.110), calls=%async_computation.5 | async-start | bytes 1048576 | tf_op jit(solution)/shard_map/all_to_all | solution.py:29
  333.5 15.2 %all-to-all-start.6 = ((f32[16,16,512]{2,1,0:T(8,128)}), f32[16,16,512]{2,1,0:T(8,128)}, u32[]{:S(2)}, u32[]{:S(2)}) async-start(f32[16,16,512]{2,1,0:T(8,128)} %broadcast_in_dim.40), calls=%async_computation.6 | async-start | bytes 1048576 | tf_op jit(solution)/shard_map/all_to_all | solution.py:41
  348.7 7.9 %copy-start.7 = (f32[1664,512]{0,1:T(8,128)S(1)}, f32[1664,512]{0,1:T(8,128)}, u32[]{:S(2)}) copy-start(f32[1664,512]{0,1:T(8,128)} %fusion.136) | copy-start | bytes 10223620
  364.6 11.1 %copy-start.2 = (f32[512,1664]{1,0:T(8,128)}, f32[512,1664]{1,0:T(8,128)S(1)}, u32[]{:S(2)}) copy-start(f32[512,1664]{1,0:T(8,128)S(1)} %bitcast_multiply_fusion.4) | copy-start | bytes 10223620
  382.5 17.9 %all-to-all-start.9 = ((f32[16,16,512]{2,1,0:T(8,128)}), f32[16,16,512]{2,1,0:T(8,128)S(1)}, u32[]{:S(2)}, u32[]{:S(2)}) async-start(f32[16,16,512]{2,1,0:T(8,128)} %reduce_sum.112), calls=%async_computation.9 | async-start | bytes 1048576 | tf_op jit(solution)/shard_map/all_to_all | solution.py:29
  401.3 13.0 %all-to-all-start.10 = ((f32[16,16,512]{2,1,0:T(8,128)}), f32[16,16,512]{2,1,0:T(8,128)S(1)}, u32[]{:S(2)}, u32[]{:S(2)}) async-start(f32[16,16,512]{2,1,0:T(8,128)} %broadcast_in_dim.43), calls=%async_computation.10 | async-start | bytes 1048576 | tf_op jit(solution)/shard_map/all_to_all | solution.py:41
  414.3 7.9 %copy-start.3 = (f32[512,1664]{1,0:T(8,128)S(1)}, f32[512,1664]{1,0:T(8,128)}, u32[]{:S(2)}) copy-start(f32[512,1664]{1,0:T(8,128)} %copy-done.2) | copy-start | bytes 10223620
  451.1 14.5 %all-to-all-start.13 = ((f32[16,16,512]{2,1,0:T(8,128)}), f32[16,16,512]{2,1,0:T(8,128)}, u32[]{:S(2)}, u32[]{:S(2)}) async-start(f32[16,16,512]{2,1,0:T(8,128)} %reduce_sum.114), calls=%async_computation.13 | async-start | bytes 1048576 | tf_op jit(solution)/shard_map/all_to_all | solution.py:29
  467.5 14.5 %all-to-all-start.14 = ((f32[16,16,512]{2,1,0:T(8,128)}), f32[16,16,512]{2,1,0:T(8,128)}, u32[]{:S(2)}, u32[]{:S(2)}) async-start(f32[16,16,512]{2,1,0:T(8,128)} %broadcast_in_dim.46), calls=%async_computation.14 | async-start | bytes 1048576 | tf_op jit(solution)/shard_map/all_to_all | solution.py:41
  482.0 8.0 %copy-start.6 = (f32[1664,512]{0,1:T(8,128)S(1)}, f32[1664,512]{0,1:T(8,128)}, u32[]{:S(2)}) copy-start(f32[1664,512]{0,1:T(8,128)} %fusion.128) | copy-start | bytes 10223620
  498.2 11.1 %copy-start = (f32[512,1664]{1,0:T(8,128)}, f32[512,1664]{1,0:T(8,128)S(1)}, u32[]{:S(2)}) copy-start(f32[512,1664]{1,0:T(8,128)S(1)} %bitcast_multiply_fusion.2) | copy-start | bytes 10223620
  516.0 17.2 %all-to-all-start.17 = ((f32[16,16,512]{2,1,0:T(8,128)}), f32[16,16,512]{2,1,0:T(8,128)S(1)}, u32[]{:S(2)}, u32[]{:S(2)}) async-start(f32[16,16,512]{2,1,0:T(8,128)} %reduce_sum.116), calls=%async_computation.17 | async-start | bytes 1048576 | tf_op jit(solution)/shard_map/all_to_all | solution.py:29
  534.1 13.4 %all-to-all-start.18 = ((f32[16,16,512]{2,1,0:T(8,128)}), f32[16,16,512]{2,1,0:T(8,128)}, u32[]{:S(2)}, u32[]{:S(2)}) async-start(f32[16,16,512]{2,1,0:T(8,128)} %broadcast_in_dim.49), calls=%async_computation.18 | async-start | bytes 1048576 | tf_op jit(solution)/shard_map/all_to_all | solution.py:41
  541.7 14.8 %copy-start.1 = (f32[512,1664]{1,0:T(8,128)S(1)}, f32[512,1664]{1,0:T(8,128)}, u32[]{:S(2)}) copy-start(f32[512,1664]{1,0:T(8,128)} %copy-done) | copy-start | bytes 10223620
  565.6 11.1 %copy-start.4 = (f32[512,1664]{1,0:T(8,128)}, f32[512,1664]{1,0:T(8,128)S(1)}, u32[]{:S(2)}) copy-start(f32[512,1664]{1,0:T(8,128)S(1)} %bitcast_multiply_fusion.1) | copy-start | bytes 10223620
  596.9 13.4 %all-to-all-start.22 = ((f32[16,16,512]{2,1,0:T(8,128)}), f32[16,16,512]{2,1,0:T(8,128)}, u32[]{:S(2)}, u32[]{:S(2)}) async-start(f32[16,16,512]{2,1,0:T(8,128)} %broadcast_in_dim.52), calls=%async_computation.22 | async-start | bytes 1048576 | tf_op jit(solution)/shard_map/all_to_all | solution.py:41
  605.0 14.3 %copy-start.5 = (f32[512,1664]{1,0:T(8,128)S(1)}, f32[512,1664]{1,0:T(8,128)}, u32[]{:S(2)}) copy-start(f32[512,1664]{1,0:T(8,128)} %copy-done.4) | copy-start | bytes 10223620
Sparse Core Ops, SparseCore 0:
  9.1 210.7 all-gather.1
where the time goes:
time: 647 us; the launch traced here: 637 us
  waiting for transfers between devices  272 us (42%)
  matrix products  145 us (22%)
  blocking collectives  87.2 us (13%)
  starting transfers between devices  53.9 us (8%)
  local copies, waits for them, and re-layouts  34.7 us (5%)
  between operations  29.6 us (5%)
  other arithmetic  14.6 us (2%)
    all_gather x1, waiting for transfers between devices, shards(): all_rows = lax.all_gather(factor, 'row', axis=1, tiled=True)  205 us
    dot_general x6, matrix products, shards(): weights = weights - jnp.dot(errors, rows_k, precision=lax.Precision.HIGHEST)  53.7 us
    all_to_all x6, blocking collectives, sent_to_all(): lax.all_to_all(jnp.broadcast_to(value[None], (devices, *value.shape)), ax...  44.3 us
    all_to_all x5, waiting for transfers between devices, summed_rows(): return jnp.sum(lax.all_to_all(own, far, 0, 0, tiled=True), axis=0)  43 us
    dot_general x36, matrix products, panel_errors(): jnp.dot(tiles[b], ublock[b * TILE:(b + 1) * TILE, a * TILE:(a + 1) * TILE...  41.5 us
    dot_general x24, matrix products, panel_errors(): jnp.dot(acc, dinv[a], precision=lax.Precision.HIGHEST)  29.7 us
    all_to_all x6, blocking collectives, sent_and_summed(): lax.all_to_all(tiles, axis, split_axis=0, concat_axis=0, tiled=True)  29.6 us
    all_to_all x5, starting transfers between devices, summed_rows(): return jnp.sum(lax.all_to_all(own, far, 0, 0, tiled=True), axis=0)  29.3 us
  transfers between devices with their start and end apart: 12, of which 10 were waited for; matrix products, arithmetic and copies ran while one was open for 6% of the time, Pallas kernels for 0%

commit v1 on v0

--- a/solution.py
+++ b/solution.py
@@ -81,7 +81,10 @@
     width = weights.shape[1]
     myself = lax.axis_index(COL)
     starts = TILE * jnp.arange(PANEL_TILES, dtype=jnp.int32)
-    all_rows = lax.all_gather(factor, "row", axis=1, tiled=True)
+    peers = lax.axis_size("row")
+    blocks = jnp.stack([factor for _ in range(peers)])
+    blocks = lax.all_to_all(blocks, "row", split_axis=0, concat_axis=0)
+    all_rows = jnp.concatenate(blocks, axis=1)
     for k in range(P_SIZE):
         first = panel_start[k]
         owner = first // width

time: 647 us -> 886 us (1.37)
  waiting for transfers between devices: 272 us -> 529 us
  matrix products: 145 us -> 124 us
  between operations: 29.6 us -> 17.2 us
    all_to_all x0 -> x1, waiting for transfers between devices: none -> 441 us  [shards(): blocks = lax.all_to_all(blocks, 'row', split_axis=0, concat_axis=0)]
    all_gather x1 -> x0, waiting for transfers between devices: 205 us -> none  [shards(): all_rows = lax.all_gather(factor, 'row', axis=1, tiled=True)]
    all_to_all x6, waiting for transfers between devices: 22.8 us -> 48 us  [sent_to_all(): lax.all_to_all(jnp.broadcast_to(value[None], (devices, *value.shape)), ax...]
    dot_general x6, matrix products: 53.7 us -> 38.1 us  [shards(): weights = weights - jnp.dot(errors, rows_k, precision=lax.Precision.HIGHEST)]
    another operation x0 -> x1, local copies, waits for them, and re-layouts: none -> 11 us  [shards(): blocks = jnp.stack([factor for _ in range(peers)])]
    all_to_all x0 -> x1, starting transfers between devices: none -> 9.13 us  [shards(): blocks = lax.all_to_all(blocks, 'row', split_axis=0, concat_axis=0)]
  transfers between devices with their start and end apart: 12 -> 12, of which waited for: 10 -> 12; matrix products, arithmetic and copies ran while one was open for 6% -> 1% of each run, Pallas kernels for 0% -> 0%
where the time goes in v1:
time: 886 us; the launch traced here: 876 us
  waiting for transfers between devices  529 us (60%)
  matrix products  124 us (14%)
  blocking collectives  89.2 us (10%)
  starting transfers between devices  59.5 us (7%)
  local copies, waits for them, and re-layouts  38.7 us (4%)
  other arithmetic  18.6 us (2%)
  between operations  17.2 us (2%)
    all_to_all x1, waiting for transfers between devices, shards(): blocks = lax.all_to_all(blocks, 'row', split_axis=0, concat_axis=0)  441 us
    all_to_all x6, waiting for transfers between devices, sent_to_all(): lax.all_to_all(jnp.broadcast_to(value[None], (devices, *value.shape)), ax...  48 us
    all_to_all x6, blocking collectives, sent_to_all(): lax.all_to_all(jnp.broadcast_to(value[None], (devices, *value.shape)), ax...  45.1 us
    dot_general x36, matrix products, panel_errors(): jnp.dot(tiles[b], ublock[b * TILE:(b + 1) * TILE, a * TILE:(a + 1) * TILE...  40.5 us
    all_to_all x5, waiting for transfers between devices, summed_rows(): return jnp.sum(lax.all_to_all(own, far, 0, 0, tiled=True), axis=0)  40.4 us
    dot_general x6, matrix products, shards(): weights = weights - jnp.dot(errors, rows_k, precision=lax.Precision.HIGHEST)  38.1 us
    all_to_all x6, blocking collectives, sent_and_summed(): lax.all_to_all(tiles, axis, split_axis=0, concat_axis=0, tiled=True)  30.8 us
    dot_general x24, matrix products, panel_errors(): jnp.dot(acc, dinv[a], precision=lax.Precision.HIGHEST)  30.4 us
  transfers between devices with their start and end apart: 12, of which 12 were waited for; matrix products, arithmetic and copies ran while one was open for 1% of the time, Pallas kernels for 0%

profile of v1, /device:TPU:1, one launch (start us, length us, event | category | flops | bytes accessed | tf_op | source)
XLA Modules:
  0.0 875.9 jit_solution(6835439854173524779)
XLA Ops:
  0.0 11.0 %stack.2 = f32[8,6,64,1664]{3,2,1,0:T(8,128)} broadcast(f32[6,64,1664]{2,1,0:T(8,128)} %param.6), dimensions={1,2,3} | broadcast | bytes 23003136 | tf_op jit(solution)/shard_map/stack | solution.py:85
  11.0 9.1 %all-to-all-start = ((f32[8,6,64,1664]{3,2,1,0:T(8,128)}), f32[8,6,64,1664]{3,2,1,0:T(8,128)}, u32[]{:S(2)}, u32[]{:S(2)}) async-start(f32[8,6,64,1664]{3,2,1,0:T(8,128)} %stack.2), calls=%async_computation | async-start | bytes 40894464 | tf_op jit(solution)/shard_map/all_to_all | solution.py:86
  25.9 440.8 %all-to-all-done = f32[8,6,64,1664]{3,2,1,0:T(8,128)} async-done(((f32[8,6,64,1664]{3,2,1,0:T(8,128)}), f32[8,6,64,1664]{3,2,1,0:T(8,128)}, u32[]{:S(2)}, u32[]{:S(2)}) %all-to-all-start) | async-done | bytes 20447264 | tf_op jit(solution)/shard_map/all_to_all | solution.py:86
  466.7 12.6 %fusion.162 = (f32[1,8,64,1664]{3,2,0,1:T(8,128)}, f32[1,8,64,1664]{3,2,0,1:T(8,128)}, f32[1,8,64,1664]{3,2,0,1:T(8,128)}, f32[1,8,64,1664]{3,2,0,1:T(8,128)}, f...) fusion(f32[6,8,64,1664]{3,2,0,1:T(8,128)} %bitcast.6), kind=kLoop, calls=%fused_computation.261 | loop fusion | bytes 40894464 | tf_op jit(solution)/shard_map/slice | solution.py:93
  497.0 6.8 all-to-all-start.2
  503.9 10.3 %all-to-all-done.2 = f32[16,16,512]{2,1,0:T(8,128)} async-done(((f32[16,16,512]{2,1,0:T(8,128)}), f32[16,16,512]{2,1,0:T(8,128)}, u32[]{:S(2)}, u32[]{:S(2)}) %all-to-all-start.2) | async-done | bytes 524320 | tf_op jit(solution)/shard_map/all_to_all | solution.py:29
  531.0 7.6 all_to_all.126
  538.7 6.4 fusion.170
  569.4 7.7 all-to-all-done.6
  584.5 8.4 all-to-all-done.7
  594.1 7.5 all_to_all.128
  637.8 7.3 all-to-all-done.10
  652.0 8.5 all-to-all-done.11
  661.8 7.6 all_to_all.130
  669.5 6.4 fusion.172
  702.8 7.7 all-to-all-done.14
  717.2 8.4 all-to-all-done.15
  726.7 7.5 all_to_all.132
  770.6 7.3 all-to-all-done.18
  784.9 8.5 all-to-all-done.19
  794.7 7.5 all_to_all.134
  828.5 13.4 %all_to_all.136 = f32[16,16,512]{2,1,0:T(8,128)S(1)} all-to-all(f32[16,16,512]{2,1,0:T(8,128)S(1)} %reduce_sum.118), channel_id=1, replica_groups=mesh['col_0'=4,'col_1'=4,'col_2'=2,'row'=8] {'col_0','col_1'}, dimensions={0} | all-to-all | bytes 1048576 | tf_op jit(solution)/shard_map/all_to_all | solution.py:29
  848.1 8.5 all-to-all-done.23
  857.8 7.5 all_to_all.137
  (188 shorter events, 224.4 us)
Async XLA Ops:
  11.0 9.1 %copy-start.15 = (s32[6]{0:T(128)S(1)}, s32[6]{0:T(128)}, u32[]{:S(2)}) copy-start(s32[6]{0:T(128)} %param.9) | copy-start | bytes 76
  11.0 12.4 %copy-start.14 = (s32[6,4,4]{0,2,1:T(4,128)S(1)}, s32[6,4,4]{0,2,1:T(4,128)}, u32[]{:S(2)}) copy-start(s32[6,4,4]{0,2,1:T(4,128)} %param.8) | copy-start | bytes 1156
  11.0 455.6 %all-to-all-start = ((f32[8,6,64,1664]{3,2,1,0:T(8,128)}), f32[8,6,64,1664]{3,2,1,0:T(8,128)}, u32[]{:S(2)}, u32[]{:S(2)}) async-start(f32[8,6,64,1664]{3,2,1,0:T(8,128)} %stack.2), calls=%async_computation | async-start | bytes 40894464 | tf_op jit(solution)/shard_map/all_to_all | solution.py:86
  466.7 12.6 %copy-start.12 = (f32[512,128]{1,0:T(8,128)S(1)}, f32[512,128]{1,0:T(8,128)}, u32[]{:S(2)}) copy-start(f32[512,128]{1,0:T(8,128)} %convolution_multiply_fusion.23) | copy-start | bytes 786436
  479.3 9.9 %copy-start.10 = (f32[1,8,64,1664]{3,2,0,1:T(8,128)}, f32[1,8,64,1664]{3,2,0,1:T(8,128)S(1)}, u32[]{:S(2)}) copy-start(f32[1,8,64,1664]{3,2,0,1:T(8,128)S(1)} %get-tuple-element.10) | copy-start | bytes 10223620
  497.0 17.3 %all-to-all-start.2 = ((f32[16,16,512]{2,1,0:T(8,128)}), f32[16,16,512]{2,1,0:T(8,128)}, u32[]{:S(2)}, u32[]{:S(2)}) async-start(f32[16,16,512]{2,1,0:T(8,128)} %reduce_sum.108), calls=%async_computation.2 | async-start | bytes 1048576 | tf_op jit(solution)/shard_map/all_to_all | solution.py:29
  516.2 13.4 %all-to-all-start.3 = ((f32[16,16,512]{2,1,0:T(8,128)}), f32[16,16,512]{2,1,0:T(8,128)}, u32[]{:S(2)}, u32[]{:S(2)}) async-start(f32[16,16,512]{2,1,0:T(8,128)} %broadcast_in_dim.37), calls=%async_computation.3 | async-start | bytes 1048576 | tf_op jit(solution)/shard_map/all_to_all | solution.py:41
  529.6 9.1 %copy-start.11 = (f32[1,8,64,1664]{3,2,0,1:T(8,128)S(1)}, f32[1,8,64,1664]{3,2,0,1:T(8,128)}, u32[]{:S(2)}) copy-start(f32[1,8,64,1664]{3,2,0,1:T(8,128)} %copy-done.10) | copy-start | bytes 10223620
  547.2 6.5 copy-start.2
  562.6 14.5 %all-to-all-start.6 = ((f32[16,16,512]{2,1,0:T(8,128)}), f32[16,16,512]{2,1,0:T(8,128)}, u32[]{:S(2)}, u32[]{:S(2)}) async-start(f32[16,16,512]{2,1,0:T(8,128)} %reduce_sum.110), calls=%async_computation.6 | async-start | bytes 1048576 | tf_op jit(solution)/shard_map/all_to_all | solution.py:29
  579.0 13.9 %all-to-all-start.7 = ((f32[16,16,512]{2,1,0:T(8,128)}), f32[16,16,512]{2,1,0:T(8,128)}, u32[]{:S(2)}, u32[]{:S(2)}) async-start(f32[16,16,512]{2,1,0:T(8,128)} %broadcast_in_dim.40), calls=%async_computation.7 | async-start | bytes 1048576 | tf_op jit(solution)/shard_map/all_to_all | solution.py:41
  630.6 14.5 %all-to-all-start.10 = ((f32[16,16,512]{2,1,0:T(8,128)}), f32[16,16,512]{2,1,0:T(8,128)}, u32[]{:S(2)}, u32[]{:S(2)}) async-start(f32[16,16,512]{2,1,0:T(8,128)} %reduce_sum.112), calls=%async_computation.10 | async-start | bytes 1048576 | tf_op jit(solution)/shard_map/all_to_all | solution.py:29
  647.0 13.5 %all-to-all-start.11 = ((f32[16,16,512]{2,1,0:T(8,128)}), f32[16,16,512]{2,1,0:T(8,128)}, u32[]{:S(2)}, u32[]{:S(2)}) async-start(f32[16,16,512]{2,1,0:T(8,128)} %broadcast_in_dim.43), calls=%async_computation.11 | async-start | bytes 1048576 | tf_op jit(solution)/shard_map/all_to_all | solution.py:41
  660.5 9.0 %copy-start.9 = (f32[1,8,64,1664]{3,2,0,1:T(8,128)S(1)}, f32[1,8,64,1664]{3,2,0,1:T(8,128)}, u32[]{:S(2)}) copy-start(f32[1,8,64,1664]{3,2,0,1:T(8,128)} %get-tuple-element.8) | copy-start | bytes 10223620
  678.0 11.7 %copy-start = (f32[512,1664]{1,0:T(8,128)}, f32[512,1664]{1,0:T(8,128)S(1)}, u32[]{:S(2)}) copy-start(f32[512,1664]{1,0:T(8,128)S(1)} %bitcast_multiply_fusion.3) | copy-start | bytes 10223620
  696.6 14.0 %all-to-all-start.14 = ((f32[16,16,512]{2,1,0:T(8,128)}), f32[16,16,512]{2,1,0:T(8,128)S(1)}, u32[]{:S(2)}, u32[]{:S(2)}) async-start(f32[16,16,512]{2,1,0:T(8,128)} %reduce_sum.114), calls=%async_computation.14 | async-start | bytes 1048576 | tf_op jit(solution)/shard_map/all_to_all | solution.py:29
  711.4 22.8 %copy-start.8 = (f32[1,8,64,1664]{3,2,0,1:T(8,128)S(1)}, f32[1,8,64,1664]{3,2,0,1:T(8,128)}, u32[]{:S(2)}) copy-start(f32[1,8,64,1664]{3,2,0,1:T(8,128)} %get-tuple-element.7) | copy-start | bytes 10223620
  711.4 14.1 %all-to-all-start.15 = ((f32[16,16,512]{2,1,0:T(8,128)}), f32[16,16,512]{2,1,0:T(8,128)}, u32[]{:S(2)}, u32[]{:S(2)}) async-start(f32[16,16,512]{2,1,0:T(8,128)} %broadcast_in_dim.46), calls=%async_computation.15 | async-start | bytes 1048576 | tf_op jit(solution)/shard_map/all_to_all | solution.py:41
  763.3 14.6 %all-to-all-start.18 = ((f32[16,16,512]{2,1,0:T(8,128)}), f32[16,16,512]{2,1,0:T(8,128)}, u32[]{:S(2)}, u32[]{:S(2)}) async-start(f32[16,16,512]{2,1,0:T(8,128)} %reduce_sum.116), calls=%async_computation.18 | async-start | bytes 1048576 | tf_op jit(solution)/shard_map/all_to_all | solution.py:29
  779.9 13.5 %all-to-all-start.19 = ((f32[16,16,512]{2,1,0:T(8,128)}), f32[16,16,512]{2,1,0:T(8,128)}, u32[]{:S(2)}, u32[]{:S(2)}) async-start(f32[16,16,512]{2,1,0:T(8,128)} %broadcast_in_dim.49), calls=%async_computation.19 | async-start | bytes 1048576 | tf_op jit(solution)/shard_map/all_to_all | solution.py:41
  793.4 8.9 %copy-start.7 = (f32[1,8,64,1664]{3,2,0,1:T(8,128)S(1)}, f32[1,8,64,1664]{3,2,0,1:T(8,128)}, u32[]{:S(2)}) copy-start(f32[1,8,64,1664]{3,2,0,1:T(8,128)} %get-tuple-element.6) | copy-start | bytes 10223620
  810.7 11.7 %copy-start.4 = (f32[512,1664]{1,0:T(8,128)}, f32[512,1664]{1,0:T(8,128)S(1)}, u32[]{:S(2)}) copy-start(f32[512,1664]{1,0:T(8,128)S(1)} %bitcast_multiply_fusion.1) | copy-start | bytes 10223620
  842.7 22.6 %copy-start.6 = (f32[1,8,64,1664]{3,2,0,1:T(8,128)S(1)}, f32[1,8,64,1664]{3,2,0,1:T(8,128)}, u32[]{:S(2)}) copy-start(f32[1,8,64,1664]{3,2,0,1:T(8,128)} %get-tuple-element.5) | copy-start | bytes 10223620
  842.7 13.9 %all-to-all-start.23 = ((f32[16,16,512]{2,1,0:T(8,128)}), f32[16,16,512]{2,1,0:T(8,128)}, u32[]{:S(2)}, u32[]{:S(2)}) async-start(f32[16,16,512]{2,1,0:T(8,128)} %broadcast_in_dim.52), calls=%async_computation.23 | async-start | bytes 1048576 | tf_op jit(solution)/shard_map/all_to_all | solution.py:41
  (4 other events, 25.5 us)
